TPU v7x, 32 devices: a whole 2x2x4 slice. The times are simulated.
32 devices in a mesh: groups: 2 (over y), replica: 1, da: 4 (over x, core), db: 4 (over z).
Axes of the slice: x: 2, y: 2, z: 4, core: 2. Of those that a mesh axis runs over, the one named last changes fastest.
Arguments:
- tokens: bfloat16 [4096, 1024], P(('groups', 'replica', 'da', 'db')), parts along dimension 0, may hold values from -6 to 6
- grad_out: bfloat16 [4096, 1024], P(('groups', 'replica', 'da', 'db')), parts along dimension 0, may hold values from -3 to 3
- routes: int32 [4096, 8], P(('groups', 'replica', 'da', 'db')), parts along dimension 0, may hold values from 0 to 15, as said below
- gates: bfloat16 [4096, 8], P(('groups', 'replica', 'da', 'db')), parts along dimension 0, may hold values from 0.019897461 to 0.5
- w_gate_up: bfloat16 [16, 1024, 768], P(('da', 'db'), 'replica'), may hold values from -0.1875 to 0.1875
- w_down: bfloat16 [16, 384, 1024], P(('da', 'db'), 'replica'), may hold values from -0.3125 to 0.3125
Outputs:
- token_grads: bfloat16 [4096, 1024], P(('groups', 'replica', 'da', 'db')), parts along dimension 0
- gate_grads: bfloat16 [4096, 8], P(('groups', 'replica', 'da', 'db')), parts along dimension 0
- gate_up_grads: bfloat16 [32, 1024, 768], P(('groups', 'da', 'db'), 'replica'), parts along dimension 0
- down_grads: bfloat16 [32, 384, 1024], P(('groups', 'da', 'db'), 'replica'), parts along dimension 0
There are 2 independent parts, one for each index of `groups`. A program takes and returns all parts, laid end to end along the dimension named above; an argument that names none is the same for every part. Nothing has to cross between parts.
Inputs may be any that keep to these rules, and one draw needn't show every extreme that they name: `routes`: each token names 8 different experts. In every aligned block of 2 consecutive tokens, each expert is named exactly once, so the tokens of one device name every expert exactly 64 times.
All inputs are finite; a program needn't handle non-finite values.
Results may differ from a plain program's by a relative error of at most 0.0085.
Values may be sent and summed in bfloat16 or wider, within the bound.
A program may use at most 64 MiB of HBM per device.

v0:
```python
import jax
import jax.numpy as jnp
from jax import lax
from jax.sharding import PartitionSpec as P


def silu_parts(projected):
    sigmoid = jax.nn.sigmoid(projected)
    return (projected * sigmoid, sigmoid * (1.0 + projected * (1.0 - sigmoid)))


def body(tokens, grad_out, routes, gates, w_gate_up, w_down):
    local_tokens, features = tokens.shape
    top_count = routes.shape[1]
    hidden_units = w_gate_up.shape[2] // 2
    first_size = lax.axis_size("da")
    second_size = lax.axis_size("db")
    experts = first_size * second_size
    per_round = experts // top_count
    rounds = local_tokens // per_round
    expert_ids = lax.broadcasted_iota(jnp.int32, (1, 1, 1, experts), 3)
    matches = routes.reshape(rounds, per_round, top_count, 1) == expert_ids
    gate_values = gates.reshape(rounds, per_round, top_count, 1).astype(jnp.float32)
    gate_table = jnp.sum(jnp.where(matches, gate_values, 0.0), axis=(1, 2)).astype(jnp.bfloat16)
    chosen = jnp.any(matches, axis=2).astype(jnp.bfloat16)
    input_send = jnp.einsum(
        "rge,rgd->red",
        chosen,
        tokens.reshape(rounds, per_round, features),
        preferred_element_type=jnp.float32,
    ).astype(jnp.bfloat16)
    upstream_send = jnp.einsum(
        "rge,rgd->red",
        chosen,
        grad_out.reshape(rounds, per_round, features),
        preferred_element_type=jnp.float32,
    ).astype(jnp.bfloat16)
    input_recv, upstream_recv, gate_recv = (
        lax.all_to_all(input_send, ("da", "db"), split_axis=1, concat_axis=1, tiled=True),
        lax.all_to_all(upstream_send, ("da", "db"), split_axis=1, concat_axis=1, tiled=True),
        lax.all_to_all(gate_table, ("da", "db"), split_axis=1, concat_axis=1, tiled=True),
    )
    input_rows = input_recv.reshape(-1, features)
    upstream_rows = upstream_recv.reshape(-1, features)
    gate_rows = gate_recv.reshape(-1, 1).astype(jnp.float32)
    w_in, w_out = (
        lax.all_gather(w_gate_up[0], "replica", axis=0, tiled=True),
        lax.all_gather(w_down[0], "replica", axis=0, tiled=True),
    )
    projected = jnp.dot(input_rows, w_in, preferred_element_type=jnp.float32)
    back_raw = jnp.einsum("rd,fd->rf", upstream_rows, w_out, preferred_element_type=jnp.float32)
    gate_part = projected[:, :hidden_units]
    up_part = projected[:, hidden_units:]
    activated, derivative = silu_parts(gate_part)
    hidden = (activated * up_part).astype(jnp.bfloat16)
    gate_scores = jnp.sum(hidden.astype(jnp.float32) * back_raw, axis=1).astype(jnp.bfloat16)
    back_hidden = gate_rows * back_raw
    grad_projected = jnp.concatenate(
        [back_hidden * up_part * derivative, back_hidden * activated], axis=1
    ).astype(jnp.bfloat16)
    scaled_upstream = (gate_rows * upstream_rows.astype(jnp.float32)).astype(jnp.bfloat16)
    input_grads = jnp.einsum("rf,df->rd", grad_projected, w_in, preferred_element_type=jnp.float32)
    input_grads = input_grads.astype(jnp.bfloat16).reshape(rounds, experts, features)
    score_back = gate_scores.reshape(rounds, experts)
    returned, score_ret = (
        lax.all_to_all(input_grads, ("da", "db"), split_axis=1, concat_axis=1, tiled=True),
        lax.all_to_all(score_back, ("da", "db"), split_axis=1, concat_axis=1, tiled=True),
    )
    score_ret = score_ret.reshape(rounds, 1, 1, experts).astype(jnp.float32)
    token_grads = (
        jnp.einsum("rge,red->rgd", chosen, returned, preferred_element_type=jnp.float32)
        .astype(jnp.bfloat16)
        .reshape(local_tokens, features)
    )
    gate_grads = (
        jnp.sum(jnp.where(matches, score_ret, 0.0), axis=3)
        .astype(jnp.bfloat16)
        .reshape(local_tokens, top_count)
    )
    columns = input_rows
    grad_in = lax.psum_scatter(
        jnp.einsum("rd,rf->df", columns, grad_projected, preferred_element_type=jnp.float32).astype(
            jnp.bfloat16
        ),
        "replica",
        scatter_dimension=0,
        tiled=True,
    )
    columns = hidden
    grad_down = lax.psum_scatter(
        jnp.einsum(
            "rf,rd->fd", columns, scaled_upstream, preferred_element_type=jnp.float32
        ).astype(jnp.bfloat16),
        "replica",
        scatter_dimension=0,
        tiled=True,
    )
    return (token_grads, gate_grads, grad_in[None], grad_down[None])


def solution(mesh):
    placed = (
        P(("groups", "replica", "da", "db"), None),
        P(("groups", "replica", "da", "db"), None),
        P(("groups", "replica", "da", "db"), None),
        P(("groups", "replica", "da", "db"), None),
        P(("da", "db"), "replica", None),
        P(("da", "db"), "replica", None),
    )
    return jax.shard_map(
        body,
        mesh=mesh,
        in_specs=placed,
        out_specs=(
            P(("groups", "replica", "da", "db"), None),
            P(("groups", "replica", "da", "db"), None),
            P(("groups", "da", "db"), "replica", None),
            P(("groups", "da", "db"), "replica", None),
        ),
        check_vma=False,
    )
```

profile of v0, /device:TPU:0, one launch (start us, length us, event | category | flops | bytes accessed | tf_op | source)
XLA Modules:
  0.0 206.5 jit_solution(12314356661567460310)
XLA Ops:
  0.6 0.9 copy.56
  1.7 0.1 copy.70
  1.8 1.1 reshape.88
  2.8 0.8 convolution_convert_fusion
  3.6 2.5 %copy.67 = bf16[64,16,1024]{2,0,1:T(8,128)(2,1)} copy(bf16[64,16,1024]{2,1,0:T(8,128)(2,1)S(1)} %convolution_convert_fusion) | data formatting | bytes 4194304 | tf_op jit(solution)/shard_map/convert_element_type | solution.py:31
  6.1 7.6 %all-to-all-start.2 = ((bf16[64,16,1024]{2,0,1:T(8,128)(2,1)}), bf16[64,16,1024]{2,0,1:T(8,128)(2,1)}, u32[]{:S(2)}, u32[]{:S(2)}) async-start(bf16[64,16,1024]{2,0,1:T(8,128)(2,1)} %copy.67), calls=%async_computation.2 | async-start | bytes 4194304 | tf_op jit(solution)/shard_map/all_to_all | solution.py:39
  13.8 0.8 convolution_convert_fusion.1
  14.6 2.5 %copy.64 = bf16[64,16,1024]{2,0,1:T(8,128)(2,1)} copy(bf16[64,16,1024]{2,1,0:T(8,128)(2,1)S(1)} %convolution_convert_fusion.1) | data formatting | bytes 4194304 | tf_op jit(solution)/shard_map/convert_element_type | solution.py:37
  17.1 45.9 %all-to-all-done.2 = bf16[64,16,1024]{2,0,1:T(8,128)(2,1)} async-done(((bf16[64,16,1024]{2,0,1:T(8,128)(2,1)}), bf16[64,16,1024]{2,0,1:T(8,128)(2,1)}, u32[]{:S(2)}, u32[]{:S(2)}) %all-to-all-start.2) | async-done | bytes 2097184 | tf_op jit(solution)/shard_map/all_to_all | solution.py:39
  63.0 4.4 %all-to-all-start.1 = ((bf16[64,16,1024]{2,0,1:T(8,128)(2,1)}), bf16[64,16,1024]{2,0,1:T(8,128)(2,1)}, u32[]{:S(2)}, u32[]{:S(2)}) async-start(bf16[64,16,1024]{2,0,1:T(8,128)(2,1)} %copy.64), calls=%async_computation.1 | async-start | bytes 4194304 | tf_op jit(solution)/shard_map/all_to_all | solution.py:40
  67.5 2.7 %copy.68 = bf16[64,16,1024]{2,1,0:T(8,128)(2,1)S(1)} copy(bf16[64,16,1024]{2,0,1:T(8,128)(2,1)} %all-to-all-done.2) | data formatting | bytes 4194304 | tf_op jit(solution)/shard_map/all_to_all | solution.py:39
  70.3 1.4 copy-done.2
  71.6 3.5 %fusion.5 = f32[1024,768]{0,1:T(8,128)} fusion(bf16[1024,1024]{1,0:T(8,128)(2,1)S(1)} %bitcast.35, bf16[1,1024,768]{2,1,0:T(8,128)(2,1)S(1)} %copy-done), kind=kOutput, calls=%fused_computation.11 | convolution fusion | flops 1610612736 | bytes 6815744 | tf_op jit(solution)/shard_map/dot_general | solution.py:50
  75.1 41.7 %all-to-all-done.1 = bf16[64,16,1024]{2,0,1:T(8,128)(2,1)} async-done(((bf16[64,16,1024]{2,0,1:T(8,128)(2,1)}), bf16[64,16,1024]{2,0,1:T(8,128)(2,1)}, u32[]{:S(2)}, u32[]{:S(2)}) %all-to-all-start.1) | async-done | bytes 2097184 | tf_op jit(solution)/shard_map/all_to_all | solution.py:40
  116.8 2.9 %copy.65 = bf16[64,16,1024]{2,1,0:T(8,128)(2,1)S(1)} copy(bf16[64,16,1024]{2,0,1:T(8,128)(2,1)} %all-to-all-done.1) | data formatting | bytes 4194304 | tf_op jit(solution)/shard_map/all_to_all | solution.py:40
  119.8 2.1 multiply_reduce_fusion
  121.9 0.7 copy.72
  122.6 3.5 %all-to-all-start.4 = ((bf16[64,16,1]{0,2,1:T(2,128)(2,1)}), bf16[64,16,1]{0,2,1:T(2,128)(2,1)S(1)}, u32[]{:S(2)}, u32[]{:S(2)}) async-start(bf16[64,16,1]{0,2,1:T(2,128)(2,1)} %copy.72), calls=%async_computation.4 | async-start | bytes 16384 | tf_op jit(solution)/shard_map/all_to_all | solution.py:67
  126.1 0.1 copy.58
  126.3 6.1 %all-to-all-done.4 = bf16[64,16,1]{0,2,1:T(2,128)(2,1)S(1)} async-done(((bf16[64,16,1]{0,2,1:T(2,128)(2,1)}), bf16[64,16,1]{0,2,1:T(2,128)(2,1)S(1)}, u32[]{:S(2)}, u32[]{:S(2)}) %all-to-all-start.4) | async-done | bytes 2080 | tf_op jit(solution)/shard_map/all_to_all | solution.py:67
  132.5 9.0 %all_to_all.27 = bf16[64,16,1]{0,2,1:T(2,128)(2,1)S(1)} all-to-all(bf16[64,16,1]{0,2,1:T(2,128)(2,1)S(1)} %copy.60), channel_id=1, replica_groups=mesh['groups'=2,'replica'=1,'da'=4,'db'=4] {'da','db'}, dimensions={1} | all-to-all | bytes 4096 | tf_op jit(solution)/shard_map/all_to_all | solution.py:41
  141.6 2.8 %multiply_convert_fusion.4 = (bf16[1024,384]{0,1:T(8,128)(2,1)S(1)}, bf16[1024,384]{0,1:T(8,128)(2,1)S(1)}) fusion(f32[1024,768]{0,1:T(8,128)} %fusion.5, f32[1024,384]{0,1:T(8,128)S(1)} %get-tuple-element.30, f32[1024]{0:T(1024)S(1)} %reshape.93), kind=kLoop, calls=%fused_computation.16 | loop fusion | flops 5505024 | bytes 6295552 | tf_op jit(solution)/shard_map/convert.3
  144.4 1.9 convolution_convert_fusion.2
  146.3 2.5 %copy.69 = bf16[64,16,1024]{2,0,1:T(8,128)(2,1)} copy(bf16[64,16,1024]{2,1,0:T(8,128)(2,1)S(1)} %bitcast.39) | data formatting | bytes 4194304 | tf_op jit(solution)/shard_map/reshape | solution.py:63
  148.8 4.6 %all-to-all-start.3 = ((bf16[64,16,1024]{2,0,1:T(8,128)(2,1)}), bf16[64,16,1024]{2,0,1:T(8,128)(2,1)}, u32[]{:S(2)}, u32[]{:S(2)}) async-start(bf16[64,16,1024]{2,0,1:T(8,128)(2,1)} %copy.69), calls=%async_computation.3 | async-start | bytes 4194304 | tf_op jit(solution)/shard_map/all_to_all | solution.py:66
  153.4 0.1 copy.73
  153.5 0.7 copy.74
  154.2 3.7 %fusion.10 = bf16[1,384,1024]{2,1,0:T(8,128)(2,1)} fusion(bf16[1024,384]{0,1:T(8,128)(2,1)S(1)} %copy-done.12, bf16[1024,1024]{1,0:T(8,128)(2,1)} %bitcast.38, f32[1024]{0:T(1024)S(1)} %reshape.93), kind=kOutput, calls=%fused_computation.21 | convolution fusion | flops 808845312 | bytes 3674112 | tf_op jit(solution)/shard_map/rf,rd->fd/dot_general | solution.py:91
  157.9 3.0 %fusion.8 = bf16[1,1024,768]{2,1,0:T(8,128)(2,1)} fusion(bf16[1024,1024]{1,0:T(8,128)(2,1)S(1)} %bitcast.36, bf16[1024,384]{0,1:T(8,128)(2,1)S(1)} %copy-done.8, bf16[1024,384]{0,1:T(8,128)(2,1)S(1)} %copy-done.6), kind=kOutput, calls=%fused_computation.19 | convolution fusion | flops 1614544896 | bytes 5242880 | tf_op jit(solution)/shard_map/rd,rf->df/dot_general | solution.py:82
  160.9 41.9 %all-to-all-done.3 = bf16[64,16,1024]{2,0,1:T(8,128)(2,1)} async-done(((bf16[64,16,1024]{2,0,1:T(8,128)(2,1)}), bf16[64,16,1024]{2,0,1:T(8,128)(2,1)}, u32[]{:S(2)}, u32[]{:S(2)}) %all-to-all-start.3) | async-done | bytes 2097184 | tf_op jit(solution)/shard_map/all_to_all | solution.py:66
  202.8 2.9 %fusion.11 = bf16[64,2,1024]{2,1,0:T(2,128)(2,1)S(1)} fusion(pred[64,2,16]{2,1,0:T(4,128)(4,1)S(1)} %copy.70, bf16[64,16,1024]{2,0,1:T(8,128)(2,1)} %all-to-all-done.3), kind=kOutput, calls=%fused_computation.22 | convolution fusion | flops 4325376 | bytes 2361344 | tf_op jit(solution)/shard_map/rge,red->rgd/dot_general | solution.py:71
  205.7 0.8 reshape.91
  (36 shorter events, 0.6 us)
Async XLA Ops:
  0.6 71.0 %copy-start = (bf16[1,1024,768]{2,1,0:T(8,128)(2,1)S(1)}, bf16[1,1024,768]{2,1,0:T(8,128)(2,1)}, u32[]{:S(2)}) copy-start(bf16[1,1024,768]{2,1,0:T(8,128)(2,1)} %param.10) | copy-start | bytes 4718596
  6.1 7.6 %copy-start.9 = (bf16[128,1024]{1,0:T(8,128)(2,1)S(1)}, bf16[128,1024]{1,0:T(8,128)(2,1)}, u32[]{:S(2)}) copy-start(bf16[128,1024]{1,0:T(8,128)(2,1)} %param.7) | copy-start | bytes 786436
  6.1 56.9 %all-to-all-start.2 = ((bf16[64,16,1024]{2,0,1:T(8,128)(2,1)}), bf16[64,16,1024]{2,0,1:T(8,128)(2,1)}, u32[]{:S(2)}, u32[]{:S(2)}) async-start(bf16[64,16,1024]{2,0,1:T(8,128)(2,1)} %copy.67), calls=%async_computation.2 | async-start | bytes 4194304 | tf_op jit(solution)/shard_map/all_to_all | solution.py:39
  63.0 53.8 %all-to-all-start.1 = ((bf16[64,16,1024]{2,0,1:T(8,128)(2,1)}), bf16[64,16,1024]{2,0,1:T(8,128)(2,1)}, u32[]{:S(2)}, u32[]{:S(2)}) async-start(bf16[64,16,1024]{2,0,1:T(8,128)(2,1)} %copy.64), calls=%async_computation.1 | async-start | bytes 4194304 | tf_op jit(solution)/shard_map/all_to_all | solution.py:40
  70.2 1.4 copy-start.2
  116.8 2.9 %copy-start.1 = (f32[1024,768]{0,1:T(8,128)S(1)}, f32[1024,768]{0,1:T(8,128)}, u32[]{:S(2)}) copy-start(f32[1024,768]{0,1:T(8,128)} %fusion.5) | copy-start | bytes 9437188
  116.8 2.9 %copy-start.11 = (bf16[1,384,1024]{2,1,0:T(8,128)(2,1)S(1)}, bf16[1,384,1024]{2,1,0:T(8,128)(2,1)}, u32[]{:S(2)}) copy-start(bf16[1,384,1024]{2,1,0:T(8,128)(2,1)} %param.11) | copy-start | bytes 2359300
  119.7 2.1 %copy-start.4 = (bf16[64,16,1024]{2,1,0:T(8,128)(2,1)}, bf16[64,16,1024]{2,1,0:T(8,128)(2,1)S(1)}, u32[]{:S(2)}) copy-start(bf16[64,16,1024]{2,1,0:T(8,128)(2,1)S(1)} %copy.65) | copy-start | bytes 6291460
  119.8 6.3 %copy-start.10 = (bf16[128,8]{0,1:T(8,128)(2,1)S(1)}, bf16[128,8]{0,1:T(8,128)(2,1)}, u32[]{:S(2)}) copy-start(bf16[128,8]{0,1:T(8,128)(2,1)} %param.9) | copy-start | bytes 6148
  122.6 9.7 %all-to-all-start.4 = ((bf16[64,16,1]{0,2,1:T(2,128)(2,1)}), bf16[64,16,1]{0,2,1:T(2,128)(2,1)S(1)}, u32[]{:S(2)}, u32[]{:S(2)}) async-start(bf16[64,16,1]{0,2,1:T(2,128)(2,1)} %copy.72), calls=%async_computation.4 | async-start | bytes 16384 | tf_op jit(solution)/shard_map/all_to_all | solution.py:67
  144.4 1.9 copy-start.5
  144.4 1.9 copy-start.7
  148.8 5.3 %copy-start.12 = (bf16[1024,384]{0,1:T(8,128)(2,1)S(1)}, bf16[1024,384]{0,1:T(8,128)(2,1)}, u32[]{:S(2)}) copy-start(bf16[1024,384]{0,1:T(8,128)(2,1)} %get-tuple-element.27) | copy-start | bytes 2359300
  148.8 53.9 %all-to-all-start.3 = ((bf16[64,16,1024]{2,0,1:T(8,128)(2,1)}), bf16[64,16,1024]{2,0,1:T(8,128)(2,1)}, u32[]{:S(2)}, u32[]{:S(2)}) async-start(bf16[64,16,1024]{2,0,1:T(8,128)(2,1)} %copy.69), calls=%async_computation.3 | async-start | bytes 4194304 | tf_op jit(solution)/shard_map/all_to_all | solution.py:66
  154.2 3.7 %copy-start.3 = (bf16[64,16,1024]{2,1,0:T(8,128)(2,1)S(1)}, bf16[64,16,1024]{2,1,0:T(8,128)(2,1)}, u32[]{:S(2)}) copy-start(bf16[64,16,1024]{2,1,0:T(8,128)(2,1)} %copy-done.2) | copy-start | bytes 6291460
  154.2 3.7 %copy-start.6 = (bf16[1024,384]{0,1:T(8,128)(2,1)S(1)}, bf16[1024,384]{0,1:T(8,128)(2,1)}, u32[]{:S(2)}) copy-start(bf16[1024,384]{0,1:T(8,128)(2,1)} %copy-done.5) | copy-start | bytes 2359300
  154.2 3.7 %copy-start.8 = (bf16[1024,384]{0,1:T(8,128)(2,1)S(1)}, bf16[1024,384]{0,1:T(8,128)(2,1)}, u32[]{:S(2)}) copy-start(bf16[1024,384]{0,1:T(8,128)(2,1)} %copy-done.7) | copy-start | bytes 2359300
where the time goes:
time: 207 us; the launch traced here: 206 us
  waiting for transfers between devices  136 us (66%)
  starting transfers between devices  20.1 us (10%)
  local copies, waits for them, and re-layouts  19.5 us (9%)
  matrix products  18.6 us (9%)
  blocking collectives  8.95 us (4%)
  other arithmetic  2.92 us (1%)
    all_to_all x1, waiting for transfers between devices, body(): lax.all_to_all(input_send, ('da', 'db'), split_axis=1, concat_axis=1, til...  45.9 us
    all_to_all x1, waiting for transfers between devices, body(): lax.all_to_all(input_grads, ('da', 'db'), split_axis=1, concat_axis=1, ti...  41.9 us
    all_to_all x1, waiting for transfers between devices, body(): lax.all_to_all(upstream_send, ('da', 'db'), split_axis=1, concat_axis=1,...  41.7 us
    all_to_all x1, blocking collectives, body(): lax.all_to_all(gate_table, ('da', 'db'), split_axis=1, concat_axis=1, til...  8.95 us
    all_to_all x1, starting transfers between devices, body(): lax.all_to_all(input_send, ('da', 'db'), split_axis=1, concat_axis=1, til...  7.57 us
    all_to_all x1, waiting for transfers between devices, body(): lax.all_to_all(score_back, ('da', 'db'), split_axis=1, concat_axis=1, til...  6.08 us
    all_to_all x1, starting transfers between devices, body(): lax.all_to_all(input_grads, ('da', 'db'), split_axis=1, concat_axis=1, ti...  4.57 us
    all_to_all x1, starting transfers between devices, body(): lax.all_to_all(upstream_send, ('da', 'db'), split_axis=1, concat_axis=1,...  4.44 us
  transfers between devices with their start and end apart: 4, of which 4 were waited for; matrix products, arithmetic and copies ran while one was open for 8% of the time, Pallas kernels for 0%

commit v1 on v0

--- a/solution.py
+++ b/solution.py
@@ -1,7 +1,15 @@
+import functools
+
 import jax
 import jax.numpy as jnp
 from jax import lax
+from jax.experimental import pallas as pl
+from jax.experimental.pallas import tpu as pltpu
 from jax.sharding import PartitionSpec as P
+
+
+CORES = 2
+MESH = pl.DeviceIdType.MESH
 
 
 def silu_parts(projected):
@@ -98,6 +106,428 @@
     return (token_grads, gate_grads, grad_in[None], grad_down[None])
 
 
+def visit(j, z, n):
+    m = jnp.minimum(z, n - 1 - z)
+    near = z + (1 - 2 * (j % 2)) * ((j + 1) // 2)
+    far = jnp.where(z < n - 1 - z, j, n - 1 - j)
+    return jnp.where(j <= 2 * m, near, far)
+
+
+def dot(a, b, dims):
+    return lax.dot_general(a, b, (dims, ((), ())), preferred_element_type=jnp.float32)
+
+
+def fused_kernel(
+    cols, depth, group,
+    tok_hbm, up_hbm, routes_ref, gates_ref, win_hbm, wout_hbm,
+    tg_ref, gg_ref, gin_ref, gdown_ref,
+    tok, up, table, win, wout, xs, su, hid, gp, igs, igb, ps, pk, pr, rs, rk, rz, scs, scr,
+    load_sem, recv_sem, zup_sem, zdn_sem, x_sem, p_sem, igs_sem, igr_sem, ps_sem, pr_sem, rs_sem, rz_sem,
+    scs_sem, scr_sem,
+):
+    da = lax.axis_index("da")
+    z = lax.axis_index("db")
+    x, c = da // CORES, da % CORES
+    local, features = tok.shape[1], tok.shape[2]
+    experts = table.shape[1]
+    top = routes_ref.shape[1]
+    rows = local // group
+    ff = wout.shape[0]
+    others = cols - 1
+
+    def slot(xx, zz, cc):
+        return (xx * CORES + cc) * depth + zz
+
+    me = slot(x, z, c)
+    loads = [
+        pltpu.make_async_copy(tok_hbm, tok.at[me], load_sem.at[0]),
+        pltpu.make_async_copy(up_hbm, up.at[me], load_sem.at[1]),
+        pltpu.make_async_copy(win_hbm.at[0], win, load_sem.at[2]),
+        pltpu.make_async_copy(wout_hbm.at[0], wout, load_sem.at[3]),
+    ]
+    for one in loads:
+        one.start()
+
+    barrier = pltpu.get_barrier_semaphore()
+    count = cols * CORES * depth
+
+    @pl.loop(1, count)
+    def _(k):
+        to = (me + k) % count
+        pl.semaphore_signal(
+            barrier, inc=1, device_id={"da": to // depth, "db": to % depth}, device_id_type=MESH
+        )
+
+    routes = routes_ref[...]
+    gates = gates_ref[...].astype(jnp.float32)
+    lanes = lax.broadcasted_iota(jnp.int32, (local, local), 1)
+    chart = jnp.zeros((local, local), jnp.float32)
+    for k in range(top):
+        chart = chart + jnp.where(routes[:, k : k + 1] == lanes, gates[:, k : k + 1], 0.0)
+    table[me] = chart.T[:experts].astype(jnp.bfloat16)
+
+    pl.semaphore_wait(barrier, count - 1)
+    loads[0].wait()
+    loads[1].wait()
+
+    held = (table, tok, up)
+
+    def send(src, dst, send_sem, recv, to_x, to_z, to_c):
+        return pltpu.make_async_remote_copy(
+            src_ref=src,
+            dst_ref=dst,
+            send_sem=send_sem,
+            recv_sem=recv,
+            device_id={"da": to_x * CORES + to_c, "db": to_z},
+            device_id_type=MESH,
+        )
+
+    def relay(s, a, sem, to_x, to_z, to_c):
+        ref = held[a].at[s]
+        return send(ref, ref, sem, recv_sem.at[s, a], to_x, to_z, to_c)
+
+    def arrive(s):
+        for a in range(3):
+            relay(s, a, p_sem.at[0, 0, a], x, z, 1 - c).wait_recv()
+
+    def spread_column(zz, act):
+        s = slot(x, zz, c)
+
+        @pl.when((zz <= z) & (z < depth - 1))
+        def _():
+            for a in range(3):
+                act(relay(s, a, zup_sem.at[zz, a], x, z + 1, c))
+
+        @pl.when((zz >= z) & (z > 0))
+        def _():
+            for a in range(3):
+                act(relay(s, a, zdn_sem.at[zz, a], x, z - 1, c))
+
+        for a in range(3):
+            for o in range(others):
+                act(relay(s, a, x_sem.at[o, zz, a], (x + 1 + o) % cols, z, c))
+        for a in range(3):
+            act(relay(s, a, p_sem.at[0, zz, a], x, z, 1 - c))
+
+    def spread_core(o, zz, act):
+        s = slot((x + 1 + o) % cols, zz, c)
+        for a in range(3):
+            act(relay(s, a, p_sem.at[1 + o, zz, a], x, z, 1 - c))
+
+    def pick(s, e):
+        chart_s = table[s].astype(jnp.float32)
+        which = lax.broadcasted_iota(jnp.int32, chart_s.shape, 0) == e
+        row = jnp.sum(jnp.where(which, chart_s, 0.0), axis=0, keepdims=True)
+        off = lax.broadcasted_iota(jnp.int32, (rows, local), 1) - group * lax.broadcasted_iota(
+            jnp.int32, (rows, local), 0
+        )
+        hit = (off >= 0) & (off < group) & (row > 0.0)
+        return jnp.where(hit, 1.0, 0.0), row
+
+    def send_ig(i, zz):
+        xx = (x + i) % cols
+        return send(
+            igs.at[xx, zz], igb.at[xx, zz, c], igs_sem.at[xx, zz], igr_sem.at[xx, zz], x, z, 1 - c
+        )
+
+    def send_score(s):
+        return pltpu.make_async_remote_copy(
+            src_ref=scs.at[s],
+            dst_ref=scr.at[me],
+            send_sem=scs_sem.at[s],
+            recv_sem=scr_sem.at[me],
+            device_id={"da": s // depth, "db": s % depth},
+            device_id_type=MESH,
+        )
+
+    def send_part(o, zz):
+        return send(
+            ps.at[o, zz],
+            pr.at[others - 1 - o, zz],
+            ps_sem.at[o, zz],
+            pr_sem.at[others - 1 - o, zz],
+            (x + 1 + o) % cols,
+            z,
+            c,
+        )
+
+    def send_row(zz):
+        return send(rs.at[zz], rz.at[z], rs_sem.at[zz], rz_sem.at[z], x, zz, c)
+
+    blocks = [(i, r) for i in range(cols) for r in range(CORES)]
+    batch = len(blocks) * rows
+
+    def compute(j, zz):
+        base = pl.multiple_of(j * batch, batch)
+        picks = []
+        gate_cols = []
+        for n, (i, r) in enumerate(blocks):
+            s = slot((x + i) % cols, zz, (c + r) % CORES)
+            chosen, row = pick(s, me)
+            picks.append((s, chosen))
+            gate_cols.append(jnp.sum(chosen * row, axis=1, keepdims=True))
+            hot = chosen.astype(jnp.bfloat16)
+            where = pl.ds(pl.multiple_of(base + n * rows, rows), rows)
+            xs[where, :] = dot(hot, tok[s], ((1,), (0,))).astype(jnp.bfloat16)
+            su[where, :] = dot(hot, up[s], ((1,), (0,))).astype(jnp.bfloat16)
+        here = pl.ds(base, batch)
+        gate = jnp.concatenate(gate_cols, axis=0)
+        upstream = su[here, :]
+        projected = dot(xs[here, :], win[...], ((1,), (0,)))
+        back_raw = dot(upstream, wout[...], ((1,), (1,)))
+        su[here, :] = (gate * upstream.astype(jnp.float32)).astype(jnp.bfloat16)
+        gate_part, up_part = projected[:, :ff], projected[:, ff:]
+        activated, derivative = silu_parts(gate_part)
+        hidden = (activated * up_part).astype(jnp.bfloat16)
+        hid[here, :] = hidden
+        scores = jnp.sum(hidden.astype(jnp.float32) * back_raw, axis=1, keepdims=True)
+        scores = scores.astype(jnp.bfloat16).astype(jnp.float32)
+        back_hidden = gate * back_raw
+        gp[here, :ff] = (back_hidden * up_part * derivative).astype(jnp.bfloat16)
+        gp[here, ff:] = (back_hidden * activated).astype(jnp.bfloat16)
+        grads = dot(gp[here, :], win[...], ((1,), (1,))).astype(jnp.bfloat16)
+        for n, (i, r) in enumerate(blocks):
+            xx = (x + i) % cols
+            piece = grads[n * rows : (n + 1) * rows]
+            if r == 0:
+                igb[xx, zz, c] = piece
+            else:
+                igs[xx, zz] = piece
+                send_ig(i, zz).start()
+        for n, (i, r) in enumerate(blocks):
+            s, chosen = picks[n]
+            line = jnp.sum(chosen * scores[n * rows : (n + 1) * rows], axis=0, keepdims=True)
+            scs[s] = jnp.broadcast_to(line, scs.shape[1:])
+            if i == 0 and r == 0:
+
+                @pl.when(zz == z)
+                def _():
+                    scr[me] = scs[me]
+
+                @pl.when(zz != z)
+                def _():
+                    send_score(s).start()
+            else:
+                send_score(s).start()
+
+    def chip_sum(i, zz):
+        xx = (x + i) % cols
+        s = slot(xx, zz, c)
+        hot = jnp.concatenate([pick(s, slot(x, z, k))[0] for k in range(CORES)], axis=0)
+        both = igb[xx, zz].reshape(CORES * rows, features)
+        return dot(hot.astype(jnp.bfloat16), both, ((0,), (0,)))
+
+    def start(copy):
+        copy.start()
+
+    def wait_send(copy):
+        copy.wait_send()
+
+    def step(i, carry):
+        @pl.when(i < depth)
+        def _():
+            zz = visit(i, z, depth)
+
+            @pl.when(i > 0)
+            def _():
+                arrive(slot(x, zz, c))
+
+            spread_column(zz, start)
+
+        @pl.when((i >= 1) & (i <= depth))
+        def _():
+            j = i - 1
+            zz = visit(j, z, depth)
+            for o in range(others):
+                arrive(slot((x + 1 + o) % cols, zz, c))
+                spread_core(o, zz, start)
+
+            @pl.when(i == 1)
+            def _():
+                loads[2].wait()
+                loads[3].wait()
+
+            for k in range(cols):
+                arrive(slot((x + k) % cols, zz, 1 - c))
+            compute(j, zz)
+            for k in list(range(1, cols)) + [0]:
+                xx = (x + k) % cols
+                send_ig(k, zz).wait_recv()
+                total = chip_sum(k, zz)
+                if k == 0:
+                    pk[zz] = total
+                else:
+                    ps[k - 1, zz] = total.astype(jnp.bfloat16)
+                    send_part(k - 1, zz).start()
+
+        @pl.when(i >= 2)
+        def _():
+            zz = visit(i - 2, z, depth)
+            total = pk[zz]
+            for o in range(others):
+                send_part(others - 1 - o, zz).wait_recv()
+                total = total + pr[o, zz].astype(jnp.float32)
+
+            @pl.when(zz == z)
+            def _():
+                rk[...] = total
+
+            @pl.when(zz != z)
+            def _():
+                rs[zz] = total.astype(jnp.bfloat16)
+                send_row(zz).start()
+
+        return carry
+
+    lax.fori_loop(0, depth + 2, step, 0)
+
+    wide = min(features, 256)
+
+    @pl.loop(0, features // wide)
+    def _(t):
+        at = pl.ds(pl.multiple_of(t * wide, wide), wide)
+        gin_ref[0, at, :] = dot(xs[:, at], gp[...], ((0,), (0,))).astype(jnp.bfloat16)
+
+    thin = 128
+
+    @pl.loop(0, ff // thin)
+    def _(t):
+        at = pl.ds(pl.multiple_of(t * thin, thin), thin)
+        gdown_ref[0, at, :] = dot(hid[:, at], su[...], ((0,), (0,))).astype(jnp.bfloat16)
+
+    @pl.loop(1, count)
+    def _(k):
+        s = (me + k) % count
+        pltpu.make_async_remote_copy(
+            src_ref=scs.at[s],
+            dst_ref=scr.at[s],
+            send_sem=scs_sem.at[s],
+            recv_sem=scr_sem.at[s],
+            device_id={"da": s // depth, "db": s % depth},
+            device_id_type=MESH,
+        ).wait()
+
+    lines = scr[:, 0, :]
+    pad = jnp.zeros((local - experts, local), jnp.float32)
+    scores = jnp.concatenate([lines, pad], axis=0).T if experts < local else lines.T
+    place = lax.broadcasted_iota(jnp.int32, (local, top), 1)
+    gate_grads = jnp.zeros((local, top), jnp.float32)
+    for k in range(top):
+        value = jnp.sum(jnp.where(routes[:, k : k + 1] == lanes, scores, 0.0), axis=1, keepdims=True)
+        gate_grads = jnp.where(place == k, value, gate_grads)
+    gg_ref[...] = gate_grads.astype(jnp.bfloat16)
+
+    def finish(k, carry):
+        zz = (z + k) % depth
+        send(rs.at[zz], rz.at[zz], rs_sem.at[zz], rz_sem.at[zz], x, zz, c).wait()
+        rk[...] += rz[zz].astype(jnp.float32)
+        return carry
+
+    lax.fori_loop(1, depth, finish, 0)
+    tg_ref[...] = rk[...].astype(jnp.bfloat16)
+
+    def drain(zz, carry):
+        spread_column(zz, wait_send)
+        for o in range(others):
+            spread_core(o, zz, wait_send)
+            send_part(o, zz).wait_send()
+        for k in range(cols):
+            send_ig(k, zz).wait_send()
+        return carry
+
+    lax.fori_loop(0, depth, drain, 0)
+
+
+def fused(tokens, grad_out, routes, gates, w_gate_up, w_down):
+    first_size, depth = lax.axis_size("da"), lax.axis_size("db")
+    cols = first_size // CORES
+    experts = first_size * depth
+    local, features = tokens.shape
+    top = routes.shape[1]
+    group = experts // top
+    rows = local // group
+    ff = w_down.shape[1]
+    bf, f32 = jnp.bfloat16, jnp.float32
+    total = rows * experts
+    dma = pltpu.SemaphoreType.DMA
+    scratch = [
+        pltpu.VMEM((experts, local, features), bf),
+        pltpu.VMEM((experts, local, features), bf),
+        pltpu.VMEM((experts, experts, local), bf),
+        pltpu.VMEM((features, 2 * ff), bf),
+        pltpu.VMEM((ff, features), bf),
+        pltpu.VMEM((total, features), bf),
+        pltpu.VMEM((total, features), bf),
+        pltpu.VMEM((total, ff), bf),
+        pltpu.VMEM((total, 2 * ff), bf),
+        pltpu.VMEM((cols, depth, rows, features), bf),
+        pltpu.VMEM((cols, depth, CORES, rows, features), bf),
+        pltpu.VMEM((cols - 1, depth, local, features), bf),
+        pltpu.VMEM((depth, local, features), f32),
+        pltpu.VMEM((cols - 1, depth, local, features), bf),
+        pltpu.VMEM((depth, local, features), bf),
+        pltpu.VMEM((local, features), f32),
+        pltpu.VMEM((depth, local, features), bf),
+        pltpu.VMEM((experts, 8, local), f32),
+        pltpu.VMEM((experts, 8, local), f32),
+        dma((4,)),
+        dma((experts, 3)),
+        dma((depth, 3)),
+        dma((depth, 3)),
+        dma((cols - 1, depth, 3)),
+        dma((cols, depth, 3)),
+        dma((cols, depth)),
+        dma((cols, depth)),
+        dma((cols - 1, depth)),
+        dma((cols - 1, depth)),
+        dma((depth,)),
+        dma((depth,)),
+        dma((experts,)),
+        dma((experts,)),
+    ]
+    vmem = pl.BlockSpec(memory_space=pltpu.VMEM)
+    hbm = pl.BlockSpec(memory_space=pl.ANY)
+    return pl.pallas_call(
+        functools.partial(fused_kernel, cols, depth, group),
+        out_shape=(
+            jax.ShapeDtypeStruct((local, features), bf),
+            jax.ShapeDtypeStruct((local, top), bf),
+            jax.ShapeDtypeStruct(w_gate_up.shape, bf),
+            jax.ShapeDtypeStruct(w_down.shape, bf),
+        ),
+        in_specs=[hbm, hbm, vmem, vmem, hbm, hbm],
+        out_specs=(vmem, vmem, vmem, vmem),
+        scratch_shapes=scratch,
+        compiler_params=pltpu.CompilerParams(
+            collective_id=0, has_side_effects=True, vmem_limit_bytes=60 * 2**20
+        ),
+    )(tokens, grad_out, routes, gates, w_gate_up, w_down)
+
+
+def fits(tokens, routes, w_down):
+    first_size = lax.axis_size("da")
+    experts = first_size * lax.axis_size("db")
+    local, features = tokens.shape
+    group = experts // routes.shape[1]
+    held = 2 * experts * local * features * 2
+    return (
+        lax.axis_size("replica") == 1
+        and first_size % CORES == 0
+        and first_size > CORES
+        and held <= 16 * 2**20
+        and local == 128
+        and experts <= local
+        and (local // group) % 16 == 0
+        and w_down.shape[1] % 128 == 0
+    )
+
+
+def route(*arrays):
+    if fits(arrays[0], arrays[2], arrays[5]):
+        return fused(*arrays)
+    return body(*arrays)
+
+
 def solution(mesh):
     placed = (
         P(("groups", "replica", "da", "db"), None),
@@ -108,7 +538,7 @@
         P(("da", "db"), "replica", None),
     )
     return jax.shard_map(
-        body,
+        route,
         mesh=mesh,
         in_specs=placed,
         out_specs=(

time: 207 us -> 109 us (0.53)
  the two profiles are of different devices: /device:TPU:0 before, /device:TPU:26 now
where the time goes in v1:
time: 109 us; the launch traced here: 108 us
  Pallas kernels  98.1 us (90%)
  local copies, waits for them, and re-layouts  9.5 us (9%)
    pallas_call x1, Pallas kernels, fused(): pl.pallas_call(functools.partial(fused_kernel, cols, depth, group), out_s...  98.1 us
    unnamed x7, local copies, waits for them, and re-layouts  8.09 us

profile of v1, /device:TPU:26, one launch (start us, length us, event | category | flops | bytes accessed | tf_op | source)
XLA Modules:
  0.0 108.3 jit_solution(7762280900227259730)
XLA Ops:
  0.6 1.4 %copy.11.gates_ref = bf16[128,8]{1,0:T(8,128)(2,1)} copy(bf16[128,8]{0,1:T(8,128)(2,1)} %param.9) | data formatting | bytes 4096 | tf_op args[3]
  2.0 1.4 %copy.10.routes_ref = s32[128,8]{1,0:T(8,128)} copy(s32[128,8]{0,1:T(8,128)} %param.8) | data formatting | bytes 8192 | tf_op args[2]
  3.4 98.1 %shard_map.93 = (bf16[128,1024]{1,0:T(8,128)(2,1)}, bf16[128,8]{1,0:T(8,128)(2,1)}, bf16[1,1024,768]{2,1,0:T(8,128)(2,1)}, bf16[1,384,1024]{2,1,0:T(8,128)(2,1)}) custom-call(bf16[128,1024]{1,0:T(8,128)(2,1)} %tok_hbm.1, bf16[128,1024]{1,0:T(8,128)(2,1)} %up_hbm.1, s32[128,8]{1,0:T(8,128)} %copy.10.routes_ref, bf16[128,8]{1,0:T(8,128)(2,1)} %copy.11.gates_ref, ...), custom_call_target="tpu_custom_call" | custom-call | tf_op jit(solution)/shard_map/pallas_call | solution.py:490
  101.6 1.4 %copy.12 = bf16[128,8]{0,1:T(8,128)(2,1)} copy(bf16[128,8]{1,0:T(8,128)(2,1)} %get-tuple-element.5) | data formatting | bytes 4096 | tf_op jit(solution)/shard_map/pallas_call | solution.py:490
  103.0 1.7 %copy.16 = bf16[128,1024]{1,0:T(8,128)(2,1)} copy(bf16[128,1024]{1,0:T(8,128)(2,1)} %get-tuple-element.12) | data formatting | bytes 524288
  104.6 0.0 copy-start
  104.6 2.7 %copy.17 = bf16[1,1024,768]{2,1,0:T(8,128)(2,1)} copy(bf16[1,1024,768]{2,1,0:T(8,128)(2,1)} %get-tuple-element.14) | data formatting | bytes 3145728
  107.4 0.0 copy-done
  107.4 0.9 copy.18
Async XLA Ops:
  104.6 2.7 %copy-start = (bf16[1,384,1024]{2,1,0:T(8,128)(2,1)S(1)}, bf16[1,384,1024]{2,1,0:T(8,128)(2,1)}, u32[]{:S(2)}) copy-start(bf16[1,384,1024]{2,1,0:T(8,128)(2,1)} %get-tuple-element.15) | copy-start | bytes 2359300

commit v2 on v1

--- a/solution.py
+++ b/solution.py
@@ -122,7 +122,7 @@
     tok_hbm, up_hbm, routes_ref, gates_ref, win_hbm, wout_hbm,
     tg_ref, gg_ref, gin_ref, gdown_ref,
     tok, up, table, win, wout, xs, su, hid, gp, igs, igb, ps, pk, pr, rs, rk, rz, scs, scr,
-    load_sem, recv_sem, zup_sem, zdn_sem, x_sem, p_sem, igs_sem, igr_sem, ps_sem, pr_sem, rs_sem, rz_sem,
+    load_sem, recv_sem, zup_sem, zdn_sem, x_sem, o_sem, p_sem, igs_sem, igr_sem, ps_sem, pr_sem, rs_sem, rz_sem,
     scs_sem, scr_sem,
 ):
     da = lax.axis_index("da")
@@ -130,7 +130,7 @@
     x, c = da // CORES, da % CORES
     local, features = tok.shape[1], tok.shape[2]
     experts = table.shape[1]
-    top = routes_ref.shape[1]
+    top = routes_ref.shape[0]
     rows = local // group
     ff = wout.shape[0]
     others = cols - 1
@@ -160,11 +160,11 @@
 
     routes = routes_ref[...]
     gates = gates_ref[...].astype(jnp.float32)
-    lanes = lax.broadcasted_iota(jnp.int32, (local, local), 1)
-    chart = jnp.zeros((local, local), jnp.float32)
+    ids = lax.broadcasted_iota(jnp.int32, (experts, local), 0)
+    chart = jnp.zeros((experts, local), jnp.float32)
     for k in range(top):
-        chart = chart + jnp.where(routes[:, k : k + 1] == lanes, gates[:, k : k + 1], 0.0)
-    table[me] = chart.T[:experts].astype(jnp.bfloat16)
+        chart = chart + jnp.where(routes[k : k + 1] == ids, gates[k : k + 1], 0.0)
+    table[me] = chart.astype(jnp.bfloat16)
 
     pl.semaphore_wait(barrier, count - 1)
     loads[0].wait()
@@ -190,6 +190,13 @@
         for a in range(3):
             relay(s, a, p_sem.at[0, 0, a], x, z, 1 - c).wait_recv()
 
+    def along(row, zz, a):
+        last = depth - 1
+        near = ((row == 1) & (zz == 0)) | ((row == last - 1) & (zz == last))
+        if a != 2:
+            return near
+        return near | ((row == 0) & (zz == last)) | ((row == last) & (zz == 0))
+
     def spread_column(zz, act):
         s = slot(x, zz, c)
 
@@ -205,12 +212,30 @@
 
         for a in range(3):
             for o in range(others):
-                act(relay(s, a, x_sem.at[o, zz, a], (x + 1 + o) % cols, z, c))
+
+                @pl.when(jnp.logical_not(along(z, zz, a)))
+                def _():
+                    act(relay(s, a, x_sem.at[o, zz, a], (x + 1 + o) % cols, z, c))
         for a in range(3):
             act(relay(s, a, p_sem.at[0, zz, a], x, z, 1 - c))
 
     def spread_core(o, zz, act):
         s = slot((x + 1 + o) % cols, zz, c)
+        last = depth - 1
+        for a in range(3):
+            up = ((z == 0) & along(1, zz, a)) | ((z == last - 1) & along(last, zz, a) & (zz == 0))
+            down = ((z == last) & along(last - 1, zz, a)) | ((z == 1) & along(0, zz, a) & (zz == last))
+            up = up & jnp.logical_not((z == 0) & (zz != 0))
+            down = down & jnp.logical_not((z == last) & (zz != last))
+
+            @pl.when(up)
+            def _():
+                act(relay(s, a, o_sem.at[o, zz, a], x, z + 1, c))
+
+            @pl.when(down)
+            def _():
+                act(relay(s, a, o_sem.at[o, zz, a], x, z - 1, c))
+
         for a in range(3):
             act(relay(s, a, p_sem.at[1 + o, zz, a], x, z, 1 - c))
 
@@ -334,15 +359,12 @@
 
             spread_column(zz, start)
 
-        @pl.when((i >= 1) & (i <= depth))
+        @pl.when((i >= 2) & (i < depth + 2))
         def _():
-            j = i - 1
+            j = i - 2
             zz = visit(j, z, depth)
-            for o in range(others):
-                arrive(slot((x + 1 + o) % cols, zz, c))
-                spread_core(o, zz, start)
-
-            @pl.when(i == 1)
+
+            @pl.when(j == 0)
             def _():
                 loads[2].wait()
                 loads[3].wait()
@@ -351,7 +373,6 @@
                 arrive(slot((x + k) % cols, zz, 1 - c))
             compute(j, zz)
             for k in list(range(1, cols)) + [0]:
-                xx = (x + k) % cols
                 send_ig(k, zz).wait_recv()
                 total = chip_sum(k, zz)
                 if k == 0:
@@ -360,9 +381,16 @@
                     ps[k - 1, zz] = total.astype(jnp.bfloat16)
                     send_part(k - 1, zz).start()
 
-        @pl.when(i >= 2)
+        @pl.when((i >= 1) & (i <= depth))
         def _():
-            zz = visit(i - 2, z, depth)
+            zz = visit(i - 1, z, depth)
+            for o in range(others):
+                arrive(slot((x + 1 + o) % cols, zz, c))
+                spread_core(o, zz, start)
+
+        @pl.when(i >= 4)
+        def _():
+            zz = visit(i - 4, z, depth)
             total = pk[zz]
             for o in range(others):
                 send_part(others - 1 - o, zz).wait_recv()
@@ -379,7 +407,7 @@
 
         return carry
 
-    lax.fori_loop(0, depth + 2, step, 0)
+    lax.fori_loop(0, depth + 4, step, 0)
 
     wide = min(features, 256)
 
@@ -407,13 +435,11 @@
             device_id_type=MESH,
         ).wait()
 
-    lines = scr[:, 0, :]
-    pad = jnp.zeros((local - experts, local), jnp.float32)
-    scores = jnp.concatenate([lines, pad], axis=0).T if experts < local else lines.T
-    place = lax.broadcasted_iota(jnp.int32, (local, top), 1)
-    gate_grads = jnp.zeros((local, top), jnp.float32)
+    scores = scr[:, 0, :]
+    place = lax.broadcasted_iota(jnp.int32, (top, local), 0)
+    gate_grads = jnp.zeros((top, local), jnp.float32)
     for k in range(top):
-        value = jnp.sum(jnp.where(routes[:, k : k + 1] == lanes, scores, 0.0), axis=1, keepdims=True)
+        value = jnp.sum(jnp.where(routes[k : k + 1] == ids, scores, 0.0), axis=0, keepdims=True)
         gate_grads = jnp.where(place == k, value, gate_grads)
     gg_ref[...] = gate_grads.astype(jnp.bfloat16)
 
@@ -475,6 +501,7 @@
         dma((depth, 3)),
         dma((depth, 3)),
         dma((cols - 1, depth, 3)),
+        dma((cols - 1, depth, 3)),
         dma((cols, depth, 3)),
         dma((cols, depth)),
         dma((cols, depth)),
@@ -486,12 +513,12 @@
         dma((experts,)),
     ]
     vmem = pl.BlockSpec(memory_space=pltpu.VMEM)
-    hbm = pl.BlockSpec(memory_space=pl.ANY)
-    return pl.pallas_call(
+    hbm = pl.BlockSpec(memory_space=pltpu.HBM)
+    token_grads, gate_grads, grad_in, grad_down = pl.pallas_call(
         functools.partial(fused_kernel, cols, depth, group),
         out_shape=(
             jax.ShapeDtypeStruct((local, features), bf),
-            jax.ShapeDtypeStruct((local, top), bf),
+            jax.ShapeDtypeStruct((top, local), bf),
             jax.ShapeDtypeStruct(w_gate_up.shape, bf),
             jax.ShapeDtypeStruct(w_down.shape, bf),
         ),
@@ -499,9 +526,11 @@
         out_specs=(vmem, vmem, vmem, vmem),
         scratch_shapes=scratch,
         compiler_params=pltpu.CompilerParams(
-            collective_id=0, has_side_effects=True, vmem_limit_bytes=60 * 2**20
+            collective_id=0, has_side_effects=True, vmem_limit_bytes=44 * 2**20
         ),
-    )(tokens, grad_out, routes, gates, w_gate_up, w_down)
+    )(*(pltpu.with_memory_space_constraint(a, pltpu.HBM) for a in (tokens, grad_out)), routes.T, gates.T,
+      *(pltpu.with_memory_space_constraint(a, pltpu.HBM) for a in (w_gate_up, w_down)))
+    return token_grads, gate_grads.T, grad_in, grad_down
 
 
 def fits(tokens, routes, w_down):
@@ -514,6 +543,7 @@
         lax.axis_size("replica") == 1
         and first_size % CORES == 0
         and first_size > CORES
+        and lax.axis_size("db") >= 4
         and held <= 16 * 2**20
         and local == 128
         and experts <= local

time: 109 us -> 91.2 us (0.84)
  the two profiles are of different devices: /device:TPU:26 before, /device:TPU:0 now
where the time goes in v2:
time: 91.2 us; the launch traced here: 91 us
  Pallas kernels  85.7 us (94%)
  local copies, waits for them, and re-layouts  4.66 us (5%)
    pallas_call x1, Pallas kernels, fused(): pl.pallas_call(functools.partial(fused_kernel, cols, depth, group), out_s...  85.7 us
    unnamed x8, local copies, waits for them, and re-layouts  4.66 us

profile of v2, /device:TPU:0, one launch (start us, length us, event | category | flops | bytes accessed | tf_op | source)
XLA Modules:
  0.0 91.0 jit_solution(14660995222305757163)
XLA Ops:
  0.6 0.0 copy-start
  0.6 0.7 copy-done
  1.3 0.0 copy-start.1
  1.3 0.7 copy-done.1
  2.0 85.7 %shard_map.93 = (bf16[128,1024]{1,0:T(8,128)(2,1)S(1)}, bf16[8,128]{1,0:T(8,128)(2,1)S(1)}, bf16[1,1024,768]{2,1,0:T(8,128)(2,1)S(1)}, bf16[1,384,1024]{2,1,0:T(8,128)(2,1)S(1)}) custom-call(bf16[128,1024]{1,0:T(8,128)(2,1)} %tok_hbm.1, bf16[128,1024]{1,0:T(8,128)(2,1)} %up_hbm.1, s32[8,128]{1,0:T(8,128)S(1)} %bitcast.3, bf16[8,128]{1,0:T(8,128)(2,1)S(1)} %bitcast.4, ...), custom_call_target="tpu_custom_call" | custom-call | tf_op jit(solution)/shard_map/pallas_call | solution.py:517
  87.7 0.7 copy.14
  88.4 0.6 copy.15
  89.0 1.1 %copy.16 = bf16[1,1024,768]{2,1,0:T(8,128)(2,1)} copy(bf16[1,1024,768]{2,1,0:T(8,128)(2,1)S(1)} %get-tuple-element.18) | data formatting | bytes 3145728
  90.1 0.9 copy.17
Async XLA Ops:
  0.6 0.7 copy-start
  1.3 0.7 copy-start.1

commit v3 on v2

--- a/solution.py
+++ b/solution.py
@@ -9,6 +9,7 @@
 
 
 CORES = 2
+PIECES = 4
 MESH = pl.DeviceIdType.MESH
 
 
@@ -119,9 +120,9 @@
 
 def fused_kernel(
     cols, depth, group,
-    tok_hbm, up_hbm, routes_ref, gates_ref, win_hbm, wout_hbm,
+    tok_hbm, up_hbm, routes_hbm, gates_hbm, win_hbm, wout_hbm,
     tg_ref, gg_ref, gin_ref, gdown_ref,
-    tok, up, table, win, wout, xs, su, hid, gp, igs, igb, ps, pk, pr, rs, rk, rz, scs, scr,
+    routes_ref, gates_ref, tok, up, table, win, wout, xs, su, hid, gp, igs, igb, ps, pk, pr, rs, rk, rz, scs, scr,
     load_sem, recv_sem, zup_sem, zdn_sem, x_sem, o_sem, p_sem, igs_sem, igr_sem, ps_sem, pr_sem, rs_sem, rz_sem,
     scs_sem, scr_sem,
 ):
@@ -144,9 +145,11 @@
         pltpu.make_async_copy(up_hbm, up.at[me], load_sem.at[1]),
         pltpu.make_async_copy(win_hbm.at[0], win, load_sem.at[2]),
         pltpu.make_async_copy(wout_hbm.at[0], wout, load_sem.at[3]),
+        pltpu.make_async_copy(routes_hbm, routes_ref, load_sem.at[4]),
+        pltpu.make_async_copy(gates_hbm, gates_ref, load_sem.at[5]),
     ]
-    for one in loads:
-        one.start()
+    for k in (4, 5, 0, 1, 2, 3):
+        loads[k].start()
 
     barrier = pltpu.get_barrier_semaphore()
     count = cols * CORES * depth
@@ -158,6 +161,8 @@
             barrier, inc=1, device_id={"da": to // depth, "db": to % depth}, device_id_type=MESH
         )
 
+    loads[4].wait()
+    loads[5].wait()
     routes = routes_ref[...]
     gates = gates_ref[...].astype(jnp.float32)
     ids = lax.broadcasted_iota(jnp.int32, (experts, local), 0)
@@ -265,19 +270,24 @@
             device_id_type=MESH,
         )
 
-    def send_part(o, zz):
+    span = local // PIECES
+
+    def part(h):
+        return pl.ds(h * span, span)
+
+    def send_part(o, zz, h):
         return send(
-            ps.at[o, zz],
-            pr.at[others - 1 - o, zz],
-            ps_sem.at[o, zz],
-            pr_sem.at[others - 1 - o, zz],
+            ps.at[o, zz, part(h)],
+            pr.at[others - 1 - o, zz, part(h)],
+            ps_sem.at[o, zz, h],
+            pr_sem.at[others - 1 - o, zz, h],
             (x + 1 + o) % cols,
             z,
             c,
         )
 
-    def send_row(zz):
-        return send(rs.at[zz], rz.at[z], rs_sem.at[zz], rz_sem.at[z], x, zz, c)
+    def send_row(zz, h):
+        return send(rs.at[zz, part(h)], rz.at[z, part(h)], rs_sem.at[zz, h], rz_sem.at[z, h], x, zz, c)
 
     blocks = [(i, r) for i in range(cols) for r in range(CORES)]
     batch = len(blocks) * rows
@@ -379,7 +389,8 @@
                     pk[zz] = total
                 else:
                     ps[k - 1, zz] = total.astype(jnp.bfloat16)
-                    send_part(k - 1, zz).start()
+                    for h in range(PIECES):
+                        send_part(k - 1, zz, h).start()
 
         @pl.when((i >= 1) & (i <= depth))
         def _():
@@ -391,19 +402,20 @@
         @pl.when(i >= 4)
         def _():
             zz = visit(i - 4, z, depth)
-            total = pk[zz]
-            for o in range(others):
-                send_part(others - 1 - o, zz).wait_recv()
-                total = total + pr[o, zz].astype(jnp.float32)
-
-            @pl.when(zz == z)
-            def _():
-                rk[...] = total
-
-            @pl.when(zz != z)
-            def _():
-                rs[zz] = total.astype(jnp.bfloat16)
-                send_row(zz).start()
+            for h in range(PIECES):
+                total = pk[zz, part(h)]
+                for o in range(others):
+                    send_part(others - 1 - o, zz, h).wait_recv()
+                    total = total + pr[o, zz, part(h)].astype(jnp.float32)
+
+                @pl.when(zz == z)
+                def _():
+                    rk[part(h), :] = total
+
+                @pl.when(zz != z)
+                def _():
+                    rs[zz, part(h)] = total.astype(jnp.bfloat16)
+                    send_row(zz, h).start()
 
         return carry
 
@@ -445,8 +457,11 @@
 
     def finish(k, carry):
         zz = (z + k) % depth
-        send(rs.at[zz], rz.at[zz], rs_sem.at[zz], rz_sem.at[zz], x, zz, c).wait()
-        rk[...] += rz[zz].astype(jnp.float32)
+        for h in range(PIECES):
+            send(
+                rs.at[zz, part(h)], rz.at[zz, part(h)], rs_sem.at[zz, h], rz_sem.at[zz, h], x, zz, c
+            ).wait()
+            rk[part(h), :] += rz[zz, part(h)].astype(jnp.float32)
         return carry
 
     lax.fori_loop(1, depth, finish, 0)
@@ -456,12 +471,37 @@
         spread_column(zz, wait_send)
         for o in range(others):
             spread_core(o, zz, wait_send)
-            send_part(o, zz).wait_send()
+            for h in range(PIECES):
+                send_part(o, zz, h).wait_send()
         for k in range(cols):
             send_ig(k, zz).wait_send()
         return carry
 
     lax.fori_loop(0, depth, drain, 0)
+
+
+def store_kernel(*refs):
+    count = len(refs) // 2
+    sems = refs[-1]
+    copies = [
+        pltpu.make_async_copy(refs[k], refs[count + k], sems.at[k]) for k in range(count)
+    ]
+    for one in copies:
+        one.start()
+    for one in copies:
+        one.wait()
+
+
+def store(*arrays):
+    anywhere = pl.BlockSpec(memory_space=pl.ANY)
+    return pl.pallas_call(
+        store_kernel,
+        out_shape=tuple(jax.ShapeDtypeStruct(a.shape, a.dtype) for a in arrays),
+        in_specs=[pl.BlockSpec(memory_space=pltpu.VMEM)] * len(arrays),
+        out_specs=(pl.BlockSpec(memory_space=pltpu.HBM),) * len(arrays),
+        scratch_shapes=[pltpu.SemaphoreType.DMA((len(arrays),))],
+        compiler_params=pltpu.CompilerParams(vmem_limit_bytes=8 * 2**20),
+    )(*arrays)
 
 
 def fused(tokens, grad_out, routes, gates, w_gate_up, w_down):
@@ -477,6 +517,8 @@
     total = rows * experts
     dma = pltpu.SemaphoreType.DMA
     scratch = [
+        pltpu.VMEM((top, local), routes.dtype),
+        pltpu.VMEM((top, local), gates.dtype),
         pltpu.VMEM((experts, local, features), bf),
         pltpu.VMEM((experts, local, features), bf),
         pltpu.VMEM((experts, experts, local), bf),
@@ -496,7 +538,7 @@
         pltpu.VMEM((depth, local, features), bf),
         pltpu.VMEM((experts, 8, local), f32),
         pltpu.VMEM((experts, 8, local), f32),
-        dma((4,)),
+        dma((6,)),
         dma((experts, 3)),
         dma((depth, 3)),
         dma((depth, 3)),
@@ -505,10 +547,10 @@
         dma((cols, depth, 3)),
         dma((cols, depth)),
         dma((cols, depth)),
-        dma((cols - 1, depth)),
-        dma((cols - 1, depth)),
-        dma((depth,)),
-        dma((depth,)),
+        dma((cols - 1, depth, PIECES)),
+        dma((cols - 1, depth, PIECES)),
+        dma((depth, PIECES)),
+        dma((depth, PIECES)),
         dma((experts,)),
         dma((experts,)),
     ]
@@ -522,14 +564,19 @@
             jax.ShapeDtypeStruct(w_gate_up.shape, bf),
             jax.ShapeDtypeStruct(w_down.shape, bf),
         ),
-        in_specs=[hbm, hbm, vmem, vmem, hbm, hbm],
+        in_specs=[hbm] * 6,
         out_specs=(vmem, vmem, vmem, vmem),
         scratch_shapes=scratch,
         compiler_params=pltpu.CompilerParams(
             collective_id=0, has_side_effects=True, vmem_limit_bytes=44 * 2**20
         ),
-    )(*(pltpu.with_memory_space_constraint(a, pltpu.HBM) for a in (tokens, grad_out)), routes.T, gates.T,
-      *(pltpu.with_memory_space_constraint(a, pltpu.HBM) for a in (w_gate_up, w_down)))
+    )(
+        *(
+            pltpu.with_memory_space_constraint(a, pltpu.HBM)
+            for a in (tokens, grad_out, routes.T, gates.T, w_gate_up, w_down)
+        )
+    )
+    token_grads, gate_grads, grad_in, grad_down = store(token_grads, gate_grads, grad_in, grad_down)
     return token_grads, gate_grads.T, grad_in, grad_down
 
 

time: 91.2 us -> 85.9 us (0.942)
  local copies, waits for them, and re-layouts: 4.66 us -> 0 us
    unnamed x8 -> x0, local copies, waits for them, and re-layouts: 4.66 us -> none
    pallas_call x1, Pallas kernels: 85.7 us -> 83.5 us  [fused(): pl.pallas_call(functools.partial(fused_kernel, cols, depth, group), out_s...]
    pallas_call x0 -> x1, Pallas kernels: none -> 1.53 us  [store(): pl.pallas_call(store_kernel, out_shape=tuple((jax.ShapeDtypeStruct(a.shap...]
where the time goes in v3:
time: 85.9 us; the launch traced here: 85.7 us
  Pallas kernels  85.1 us (99%)
    pallas_call x1, Pallas kernels, fused(): pl.pallas_call(functools.partial(fused_kernel, cols, depth, group), out_s...  83.5 us

profile of v3, /device:TPU:0, one launch (start us, length us, event | category | flops | bytes accessed | tf_op | source)
XLA Modules:
  0.0 85.7 jit_solution(524704061354076374)
XLA Ops:
  0.6 83.5 %shard_map.93 = (bf16[128,1024]{1,0:T(8,128)(2,1)S(1)}, bf16[8,128]{1,0:T(8,128)(2,1)S(1)}, bf16[1,1024,768]{2,1,0:T(8,128)(2,1)S(1)}, bf16[1,384,1024]{2,1,0:T(8,128)(2,1)S(1)}) custom-call(bf16[128,1024]{1,0:T(8,128)(2,1)} %tok_hbm.1, bf16[128,1024]{1,0:T(8,128)(2,1)} %up_hbm.1, s32[8,128]{1,0:T(8,128)} %bitcast.3, bf16[8,128]{1,0:T(8,128)(2,1)} %bitcast.4, ...), custom_call_target="tpu_custom_call" | custom-call | tf_op jit(solution)/shard_map/pallas_call | solution.py:559
  84.2 1.5 %shard_map.94 = (bf16[128,1024]{1,0:T(8,128)(2,1)}, bf16[8,128]{1,0:T(8,128)(2,1)}, bf16[1,1024,768]{2,1,0:T(8,128)(2,1)}, bf16[1,384,1024]{2,1,0:T(8,128)(2,1)}) custom-call(bf16[128,1024]{1,0:T(8,128)(2,1)S(1)} %get-tuple-element.12.refs_0_, bf16[8,128]{1,0:T(8,128)(2,1)S(1)} %get-tuple-element.13.refs_1_, ...), custom_call_target="tpu_custom_call" | custom-call | tf_op jit(solution)/shard_map/pallas_call | solution.py:497

commit v4 on v3

--- a/solution.py
+++ b/solution.py
@@ -202,26 +202,29 @@
             return near
         return near | ((row == 0) & (zz == last)) | ((row == last) & (zz == 0))
 
-    def spread_column(zz, act):
+    def spread_column(zz, act, await_first=None):
         s = slot(x, zz, c)
-
-        @pl.when((zz <= z) & (z < depth - 1))
-        def _():
-            for a in range(3):
+        for a in range(3):
+            if await_first is not None:
+
+                @pl.when(await_first)
+                def _():
+                    relay(s, a, p_sem.at[0, 0, a], x, z, 1 - c).wait_recv()
+
+            @pl.when((zz <= z) & (z < depth - 1))
+            def _():
                 act(relay(s, a, zup_sem.at[zz, a], x, z + 1, c))
 
-        @pl.when((zz >= z) & (z > 0))
-        def _():
-            for a in range(3):
+            @pl.when((zz >= z) & (z > 0))
+            def _():
                 act(relay(s, a, zdn_sem.at[zz, a], x, z - 1, c))
 
-        for a in range(3):
             for o in range(others):
 
                 @pl.when(jnp.logical_not(along(z, zz, a)))
                 def _():
                     act(relay(s, a, x_sem.at[o, zz, a], (x + 1 + o) % cols, z, c))
-        for a in range(3):
+
             act(relay(s, a, p_sem.at[0, zz, a], x, z, 1 - c))
 
     def spread_core(o, zz, act):
@@ -363,11 +366,7 @@
         def _():
             zz = visit(i, z, depth)
 
-            @pl.when(i > 0)
-            def _():
-                arrive(slot(x, zz, c))
-
-            spread_column(zz, start)
+            spread_column(zz, start, i > 0)
 
         @pl.when((i >= 2) & (i < depth + 2))
         def _():

time: 85.9 us -> 84 us (0.978)
  Pallas kernels: 85.1 us -> 83.2 us
    pallas_call x1, Pallas kernels: 83.5 us -> 81.7 us  [fused(): pl.pallas_call(functools.partial(fused_kernel, cols, depth, group), out_s...]
where the time goes in v4:
time: 84 us; the launch traced here: 83.8 us
  Pallas kernels  83.2 us (99%)
    pallas_call x1, Pallas kernels, fused(): pl.pallas_call(functools.partial(fused_kernel, cols, depth, group), out_s...  81.7 us

profile of v4, /device:TPU:0, one launch (start us, length us, event | category | flops | bytes accessed | tf_op | source)
XLA Modules:
  0.0 83.8 jit_solution(10295013746316000547)
XLA Ops:
  0.6 81.7 %shard_map.93 = (bf16[128,1024]{1,0:T(8,128)(2,1)S(1)}, bf16[8,128]{1,0:T(8,128)(2,1)S(1)}, bf16[1,1024,768]{2,1,0:T(8,128)(2,1)S(1)}, bf16[1,384,1024]{2,1,0:T(8,128)(2,1)S(1)}) custom-call(bf16[128,1024]{1,0:T(8,128)(2,1)} %tok_hbm.1, bf16[128,1024]{1,0:T(8,128)(2,1)} %up_hbm.1, s32[8,128]{1,0:T(8,128)} %bitcast.3, bf16[8,128]{1,0:T(8,128)(2,1)} %bitcast.4, ...), custom_call_target="tpu_custom_call" | custom-call | tf_op jit(solution)/shard_map/pallas_call | solution.py:558
  82.3 1.5 %shard_map.94 = (bf16[128,1024]{1,0:T(8,128)(2,1)}, bf16[8,128]{1,0:T(8,128)(2,1)}, bf16[1,1024,768]{2,1,0:T(8,128)(2,1)}, bf16[1,384,1024]{2,1,0:T(8,128)(2,1)}) custom-call(bf16[128,1024]{1,0:T(8,128)(2,1)S(1)} %get-tuple-element.12.refs_0_, bf16[8,128]{1,0:T(8,128)(2,1)S(1)} %get-tuple-element.13.refs_1_, ...), custom_call_target="tpu_custom_call" | custom-call | tf_op jit(solution)/shard_map/pallas_call | solution.py:496
